TPU v7x, 256 devices: a whole 4x4x8 slice. The times are simulated.
256 devices in a mesh: row: 32 (over x, z_hi, y), col: 8 (over z_lo, core).
Axes of the slice: x: 4, y: 4, z: 8 (z_hi: 2, z_lo: 4; z = z_hi * 4 + z_lo), core: 2. Of those that a mesh axis runs over, the one named last changes fastest.
Arguments:
- coupling: float32 [24576, 24576], P('row', 'col'), may hold values from -1 to 5, as said below
- vectors: float32 [24576, 256], P(('row', 'col')), may hold values from -6 to 6
Outputs:
- filtered: float32 [24576, 256], P(('row', 'col'))
- gram: float32 [256, 256], replicated
Inputs may be any that keep to these rules, and one draw needn't show every extreme that they name: `coupling`: H, the operator with its column order restored, is symmetric.
All inputs are finite; a program needn't handle non-finite values.
Results may differ from a plain program's by a relative error of at most 0.0001.
Values sent between devices are 32-bit elements; how exact they have to be, the bound alone decides.
No kernel may reach another device: no remote copies, remote signals or barrier semaphores. Data moves between devices by JAX's collectives and lax.ppermute only.
A program may use at most 64 MiB of HBM per device.

v0:
```python
import jax
import jax.numpy as jnp
from jax import lax
from jax.sharding import PartitionSpec as P

ORDER = 24576
DEGREE = 6
filter_center = 2.75
filter_half = 1.75
filter_lower = 0.0


def on_device(coupling, vectors):

    def operate(current):
        partial_value = jnp.dot(
            coupling,
            lax.all_gather(current, "row", axis=0, tiled=True),
            precision=lax.Precision.HIGHEST,
            preferred_element_type=jnp.float32,
        )
        product = lax.psum_scatter(partial_value, "col", scatter_dimension=0, tiled=True)
        return product - filter_center * current

    sigma_first = filter_half / (filter_lower - filter_center)
    previous = vectors
    current = sigma_first / filter_half * operate(vectors)
    sigma_now = sigma_first
    for degree_index in range(DEGREE - 1):
        sigma_new = 1.0 / (2.0 / sigma_first - sigma_now)
        following = (
            2.0 * sigma_new / filter_half * operate(current) - sigma_now * sigma_new * previous
        )
        previous = current
        current = following
        sigma_now = sigma_new
    local_gram = jnp.dot(
        current.T, current, precision=lax.Precision.HIGHEST, preferred_element_type=jnp.float32
    )
    gram = lax.psum(local_gram, ("row", "col")) / ORDER
    return (current, gram)


def solution(mesh):
    return jax.shard_map(
        on_device,
        mesh=mesh,
        in_specs=(P("row", "col"), P(("row", "col"), None)),
        out_specs=(P(("row", "col"), None), P()),
        check_vma=False,
    )
```

profile of v0, /device:TPU:2, one launch (start us, length us, event | category | flops | bytes accessed | tf_op | source)
XLA Modules:
  0.0 1155.9 jit_solution(2117309607729727020)
XLA Ops:
  8.0 105.9 %all-gather.7.cloned.1.call-done = f32[3072,256]{1,0:T(8,128)} async-done(((f32[96,256]{1,0:T(8,128)}), f32[3072,256]{1,0:T(8,128)}) %all-gather.7.cloned.1.call-update) | async-done | bytes 3145744 | tf_op jit(solution)/shard_map/all_gather | solution.py:18
  113.9 11.4 fusion
  125.4 32.3 %reduce-scatter.7.cloned.1.call-done = f32[96,256]{1,0:T(8,128)} async-done(((f32[768,256]{1,0:T(8,128)}), f32[96,256]{1,0:T(8,128)}) %reduce-scatter.7.cloned.1.call-update) | async-done | bytes 98320 | tf_op jit(solution)/shard_map/reduce_scatter | solution.py:22
  159.4 100.7 %all-gather.9.cloned.1.call-done = f32[3072,256]{1,0:T(8,128)} async-done(((f32[96,256]{1,0:T(8,128)}), f32[3072,256]{1,0:T(8,128)}) %all-gather.9.cloned.1.call-update) | async-done | bytes 3145744 | tf_op jit(solution)/shard_map/all_gather | solution.py:18
  260.1 11.4 convolution_bitcast_fusion.4
  271.6 32.3 %reduce-scatter.9.cloned.1.call-done = f32[96,256]{1,0:T(8,128)} async-done(((f32[768,256]{1,0:T(8,128)}), f32[96,256]{1,0:T(8,128)}) %reduce-scatter.9.cloned.1.call-update) | async-done | bytes 98320 | tf_op jit(solution)/shard_map/reduce_scatter | solution.py:22
  303.9 1.6 multiply_subtract_fusion.4
  305.7 100.4 %all-gather.11.cloned.1.call-done = f32[3072,256]{1,0:T(8,128)} async-done(((f32[96,256]{1,0:T(8,128)}), f32[3072,256]{1,0:T(8,128)}) %all-gather.11.cloned.1.call-update) | async-done | bytes 3145744 | tf_op jit(solution)/shard_map/all_gather | solution.py:18
  406.1 11.4 convolution_bitcast_fusion.3
  417.7 32.3 %reduce-scatter.11.cloned.1.call-done = f32[96,256]{1,0:T(8,128)} async-done(((f32[768,256]{1,0:T(8,128)}), f32[96,256]{1,0:T(8,128)}) %reduce-scatter.11.cloned.1.call-update) | async-done | bytes 98320 | tf_op jit(solution)/shard_map/reduce_scatter | solution.py:22
  450.0 1.6 multiply_subtract_fusion.3
  451.6 100.7 %all-gather.13.cloned.1.call-done = f32[3072,256]{1,0:T(8,128)} async-done(((f32[96,256]{1,0:T(8,128)}), f32[3072,256]{1,0:T(8,128)}) %all-gather.13.cloned.1.call-update) | async-done | bytes 3145744 | tf_op jit(solution)/shard_map/all_gather | solution.py:18
  552.4 11.4 convolution_bitcast_fusion.2
  563.9 32.3 %reduce-scatter.13.cloned.1.call-done = f32[96,256]{1,0:T(8,128)} async-done(((f32[768,256]{1,0:T(8,128)}), f32[96,256]{1,0:T(8,128)}) %reduce-scatter.13.cloned.1.call-update) | async-done | bytes 98320 | tf_op jit(solution)/shard_map/reduce_scatter | solution.py:22
  596.2 1.6 multiply_subtract_fusion.2
  598.1 100.5 %all-gather.15.cloned.1.call-done = f32[3072,256]{1,0:T(8,128)} async-done(((f32[96,256]{1,0:T(8,128)}), f32[3072,256]{1,0:T(8,128)}) %all-gather.15.cloned.1.call-update) | async-done | bytes 3145744 | tf_op jit(solution)/shard_map/all_gather | solution.py:18
  698.6 11.4 convolution_bitcast_fusion.1
  710.2 32.3 %reduce-scatter.15.cloned.1.call-done = f32[96,256]{1,0:T(8,128)} async-done(((f32[768,256]{1,0:T(8,128)}), f32[96,256]{1,0:T(8,128)}) %reduce-scatter.15.cloned.1.call-update) | async-done | bytes 98320 | tf_op jit(solution)/shard_map/reduce_scatter | solution.py:22
  742.5 1.6 multiply_subtract_fusion.1
  744.1 100.7 %all-gather.17.cloned.1.call-done = f32[3072,256]{1,0:T(8,128)} async-done(((f32[96,256]{1,0:T(8,128)}), f32[3072,256]{1,0:T(8,128)}) %all-gather.17.cloned.1.call-update) | async-done | bytes 3145744 | tf_op jit(solution)/shard_map/all_gather | solution.py:18
  844.8 11.4 convolution_bitcast_fusion
  856.3 32.3 %reduce-scatter.17.cloned.1.call-done = f32[96,256]{1,0:T(8,128)} async-done(((f32[768,256]{1,0:T(8,128)}), f32[96,256]{1,0:T(8,128)}) %reduce-scatter.17.cloned.1.call-update) | async-done | bytes 98320 | tf_op jit(solution)/shard_map/reduce_scatter | solution.py:22
  890.8 257.0 %all-reduce.2.cloned.1.call-done = f32[256,256]{1,0:T(8,128)} async-done(((f32[256,256]{1,0:T(8,128)}), f32[256,256]{1,0:T(8,128)}) %all-reduce.2.cloned.1.call-update) | async-done | bytes 262160 | tf_op jit(solution)/shard_map/psum | solution.py:40
  1147.7 1.7 broadcast_multiply_fusion
  (43 shorter events, 5.4 us)
Async XLA Ops:
  7.2 106.7 %all-gather.7.cloned.1.call-start = ((), (), s32[]{:S(2)}) async-start(), calls=%async_computation.6 | async-start | bytes 3244032 | tf_op jit(solution)/shard_map/all_gather | solution.py:18
  7.9 149.8 %copy-start = (f32[96,256]{1,0:T(8,128)S(1)}, f32[96,256]{1,0:T(8,128)}, u32[]{:S(2)}) copy-start(f32[96,256]{1,0:T(8,128)} %param.3) | copy-start | bytes 294916
  7.9 149.8 %reduce-scatter.7.cloned.1.call-start = ((), (), s32[]{:S(2)}) async-start(), calls=%async_computation.7 | async-start | bytes 884736 | tf_op jit(solution)/shard_map/reduce_scatter | solution.py:22
  125.3 134.7 %all-gather.9.cloned.1.call-start = ((), (), s32[]{:S(2)}) async-start(), calls=%async_computation.8 | async-start | bytes 3244032 | tf_op jit(solution)/shard_map/all_gather | solution.py:18
  159.3 144.6 %copy-start.6 = (f32[96,256]{1,0:T(8,128)S(1)}, f32[96,256]{1,0:T(8,128)}, u32[]{:S(2)}) copy-start(f32[96,256]{1,0:T(8,128)} %reduce-scatter.7.cloned.1.call-done) | copy-start | bytes 294916
  159.3 144.6 %reduce-scatter.9.cloned.1.call-start = ((), (), s32[]{:S(2)}) async-start(), calls=%async_computation.9 | async-start | bytes 884736 | tf_op jit(solution)/shard_map/reduce_scatter | solution.py:22
  271.5 134.6 %all-gather.11.cloned.1.call-start = ((), (), s32[]{:S(2)}) async-start(), calls=%async_computation.10 | async-start | bytes 3244032 | tf_op jit(solution)/shard_map/all_gather | solution.py:18
  305.5 144.5 %copy-start.3 = (f32[96,256]{1,0:T(8,128)S(1)}, f32[96,256]{1,0:T(8,128)}, u32[]{:S(2)}) copy-start(f32[96,256]{1,0:T(8,128)} %multiply_subtract_fusion.4) | copy-start | bytes 294916
  305.5 144.5 %reduce-scatter.11.cloned.1.call-start = ((), (), s32[]{:S(2)}) async-start(), calls=%async_computation.11 | async-start | bytes 884736 | tf_op jit(solution)/shard_map/reduce_scatter | solution.py:22
  417.6 134.8 %all-gather.13.cloned.1.call-start = ((), (), s32[]{:S(2)}) async-start(), calls=%async_computation.12 | async-start | bytes 3244032 | tf_op jit(solution)/shard_map/all_gather | solution.py:18
  451.6 144.6 %copy-start.1 = (f32[96,256]{1,0:T(8,128)S(1)}, f32[96,256]{1,0:T(8,128)}, u32[]{:S(2)}) copy-start(f32[96,256]{1,0:T(8,128)} %multiply_subtract_fusion.3) | copy-start | bytes 294916
  451.6 144.6 %reduce-scatter.13.cloned.1.call-start = ((), (), s32[]{:S(2)}) async-start(), calls=%async_computation.13 | async-start | bytes 884736 | tf_op jit(solution)/shard_map/reduce_scatter | solution.py:22
  563.8 134.8 %all-gather.15.cloned.1.call-start = ((), (), s32[]{:S(2)}) async-start(), calls=%async_computation.14 | async-start | bytes 3244032 | tf_op jit(solution)/shard_map/all_gather | solution.py:18
  597.8 144.7 %copy-start.2 = (f32[96,256]{1,0:T(8,128)S(1)}, f32[96,256]{1,0:T(8,128)}, u32[]{:S(2)}) copy-start(f32[96,256]{1,0:T(8,128)} %multiply_subtract_fusion.2) | copy-start | bytes 294916
  597.8 144.7 %reduce-scatter.15.cloned.1.call-start = ((), (), s32[]{:S(2)}) async-start(), calls=%async_computation.15 | async-start | bytes 884736 | tf_op jit(solution)/shard_map/reduce_scatter | solution.py:22
  710.1 134.7 %all-gather.17.cloned.1.call-start = ((), (), s32[]{:S(2)}) async-start(), calls=%async_computation.16 | async-start | bytes 3244032 | tf_op jit(solution)/shard_map/all_gather | solution.py:18
  744.1 144.6 %copy-start.5 = (f32[96,256]{1,0:T(8,128)S(1)}, f32[96,256]{1,0:T(8,128)}, u32[]{:S(2)}) copy-start(f32[96,256]{1,0:T(8,128)} %multiply_subtract_fusion.1) | copy-start | bytes 294916
  744.1 144.6 %reduce-scatter.17.cloned.1.call-start = ((), (), s32[]{:S(2)}) async-start(), calls=%async_computation.17 | async-start | bytes 884736 | tf_op jit(solution)/shard_map/reduce_scatter | solution.py:22
  856.3 291.4 %all-reduce.2.cloned.1.call-start = ((), (), s32[]{:S(2)}) async-start(), calls=%async_computation.18 | async-start | bytes 524288 | tf_op jit(solution)/shard_map/psum | solution.py:40
  889.6 259.8 %copy-start.4 = (f32[96,256]{1,0:T(8,128)}, f32[96,256]{1,0:T(8,128)S(1)}, u32[]{:S(2)}) copy-start(f32[96,256]{1,0:T(8,128)S(1)} %multiply_subtract_fusion) | copy-start | bytes 294916
Sparse Core Ops, SparseCore 0:
  11.4 102.4 all-gather.6
  125.4 32.2 reduce-scatter.6
  161.7 98.3 all-gather.8
  271.6 32.2 reduce-scatter.8
  307.7 98.3 all-gather.10
  417.7 32.2 reduce-scatter.10
  454.0 98.3 all-gather.12
  564.0 32.2 reduce-scatter.12
  600.2 98.3 all-gather.14
  710.2 32.2 reduce-scatter.14
  746.5 98.3 all-gather.16
  856.4 32.2 reduce-scatter.16
  894.7 252.9 all-reduce.1
where the time goes:
time: 1160 us
  waiting for transfers between devices  1060 us (91%)
  matrix products  69.7 us (6%)
  between operations  14 us (1%)
    all_gather x6, waiting for transfers between devices, operate(): lax.all_gather(current, 'row', axis=0, tiled=True)  609 us
    psum x1, waiting for transfers between devices, on_device(): gram = lax.psum(local_gram, ('row', 'col')) / ORDER  257 us
    reduce_scatter x6, waiting for transfers between devices, operate(): lax.psum_scatter(partial_value, 'col', scatter_dimension=0, tiled=True)  194 us
    dot_general x6, matrix products, operate(): jnp.dot(coupling, lax.all_gather(current, 'row', axis=0, tiled=True), pre...  68.6 us
  transfers between devices with their start and end apart: 13, of which 13 were waited for; matrix products, arithmetic and copies ran while one was open for 0% of the time, Pallas kernels for 0%

commit v1 on v0

--- a/solution.py
+++ b/solution.py
@@ -8,6 +8,11 @@
 filter_center = 2.75
 filter_half = 1.75
 filter_lower = 0.0
+
+
+def one_after_other(array, first, second):
+    partial = lax.psum(array, first)
+    return lax.psum(partial, second)
 
 
 def on_device(coupling, vectors):
@@ -37,7 +42,7 @@
     local_gram = jnp.dot(
         current.T, current, precision=lax.Precision.HIGHEST, preferred_element_type=jnp.float32
     )
-    gram = lax.psum(local_gram, ("row", "col")) / ORDER
+    gram = one_after_other(local_gram, "row", "col") / ORDER
     return (current, gram)
 
 

time: 1160 us -> 1400 us (1.21)
  waiting for transfers between devices: 1060 us -> 1300 us
    psum x1 -> x2, waiting for transfers between devices: 257 us -> 501 us  [the longest x1 411 us: one_after_other(): partial = lax.psum(array, first)]
  transfers between devices with their start and end apart: 13 -> 14, of which waited for: 13 -> 14; matrix products, arithmetic and copies ran while one was open for 0% -> 0% of each run, Pallas kernels for 0% -> 0%
where the time goes in v1:
time: 1400 us
  waiting for transfers between devices  1300 us (93%)
  matrix products  69.7 us (5%)
  between operations  14 us (1%)
    all_gather x6, waiting for transfers between devices, operate(): lax.all_gather(current, 'row', axis=0, tiled=True)  609 us
    psum x1, waiting for transfers between devices, one_after_other(): partial = lax.psum(array, first)  411 us
    reduce_scatter x6, waiting for transfers between devices, operate(): lax.psum_scatter(partial_value, 'col', scatter_dimension=0, tiled=True)  194 us
    psum x1, waiting for transfers between devices, one_after_other(): return lax.psum(partial, second)  89.6 us
    dot_general x6, matrix products, operate(): jnp.dot(coupling, lax.all_gather(current, 'row', axis=0, tiled=True), pre...  68.6 us
  transfers between devices with their start and end apart: 14, of which 14 were waited for; matrix products, arithmetic and copies ran while one was open for 0% of the time, Pallas kernels for 0%

profile of v1, /device:TPU:2, one launch (start us, length us, event | category | flops | bytes accessed | tf_op | source)
XLA Modules:
  0.0 1399.6 jit_solution(2903275294222887304)
XLA Ops:
  8.0 105.9 %all-gather.7.cloned.1.call-done = f32[3072,256]{1,0:T(8,128)} async-done(((f32[96,256]{1,0:T(8,128)}), f32[3072,256]{1,0:T(8,128)}) %all-gather.7.cloned.1.call-update) | async-done | bytes 3145744 | tf_op jit(solution)/shard_map/all_gather | solution.py:23
  113.9 11.4 fusion
  125.4 32.3 %reduce-scatter.7.cloned.1.call-done = f32[96,256]{1,0:T(8,128)} async-done(((f32[768,256]{1,0:T(8,128)}), f32[96,256]{1,0:T(8,128)}) %reduce-scatter.7.cloned.1.call-update) | async-done | bytes 98320 | tf_op jit(solution)/shard_map/reduce_scatter | solution.py:27
  159.4 100.7 %all-gather.9.cloned.1.call-done = f32[3072,256]{1,0:T(8,128)} async-done(((f32[96,256]{1,0:T(8,128)}), f32[3072,256]{1,0:T(8,128)}) %all-gather.9.cloned.1.call-update) | async-done | bytes 3145744 | tf_op jit(solution)/shard_map/all_gather | solution.py:23
  260.1 11.4 convolution_bitcast_fusion.4
  271.6 32.3 %reduce-scatter.9.cloned.1.call-done = f32[96,256]{1,0:T(8,128)} async-done(((f32[768,256]{1,0:T(8,128)}), f32[96,256]{1,0:T(8,128)}) %reduce-scatter.9.cloned.1.call-update) | async-done | bytes 98320 | tf_op jit(solution)/shard_map/reduce_scatter | solution.py:27
  303.9 1.6 multiply_subtract_fusion.4
  305.7 100.4 %all-gather.11.cloned.1.call-done = f32[3072,256]{1,0:T(8,128)} async-done(((f32[96,256]{1,0:T(8,128)}), f32[3072,256]{1,0:T(8,128)}) %all-gather.11.cloned.1.call-update) | async-done | bytes 3145744 | tf_op jit(solution)/shard_map/all_gather | solution.py:23
  406.1 11.4 convolution_bitcast_fusion.3
  417.7 32.3 %reduce-scatter.11.cloned.1.call-done = f32[96,256]{1,0:T(8,128)} async-done(((f32[768,256]{1,0:T(8,128)}), f32[96,256]{1,0:T(8,128)}) %reduce-scatter.11.cloned.1.call-update) | async-done | bytes 98320 | tf_op jit(solution)/shard_map/reduce_scatter | solution.py:27
  450.0 1.6 multiply_subtract_fusion.3
  451.6 100.7 %all-gather.13.cloned.1.call-done = f32[3072,256]{1,0:T(8,128)} async-done(((f32[96,256]{1,0:T(8,128)}), f32[3072,256]{1,0:T(8,128)}) %all-gather.13.cloned.1.call-update) | async-done | bytes 3145744 | tf_op jit(solution)/shard_map/all_gather | solution.py:23
  552.4 11.4 convolution_bitcast_fusion.2
  563.9 32.3 %reduce-scatter.13.cloned.1.call-done = f32[96,256]{1,0:T(8,128)} async-done(((f32[768,256]{1,0:T(8,128)}), f32[96,256]{1,0:T(8,128)}) %reduce-scatter.13.cloned.1.call-update) | async-done | bytes 98320 | tf_op jit(solution)/shard_map/reduce_scatter | solution.py:27
  596.2 1.6 multiply_subtract_fusion.2
  598.1 100.5 %all-gather.15.cloned.1.call-done = f32[3072,256]{1,0:T(8,128)} async-done(((f32[96,256]{1,0:T(8,128)}), f32[3072,256]{1,0:T(8,128)}) %all-gather.15.cloned.1.call-update) | async-done | bytes 3145744 | tf_op jit(solution)/shard_map/all_gather | solution.py:23
  698.6 11.4 convolution_bitcast_fusion.1
  710.2 32.3 %reduce-scatter.15.cloned.1.call-done = f32[96,256]{1,0:T(8,128)} async-done(((f32[768,256]{1,0:T(8,128)}), f32[96,256]{1,0:T(8,128)}) %reduce-scatter.15.cloned.1.call-update) | async-done | bytes 98320 | tf_op jit(solution)/shard_map/reduce_scatter | solution.py:27
  744.1 100.7 %all-gather.17.cloned.1.call-done = f32[3072,256]{1,0:T(8,128)} async-done(((f32[96,256]{1,0:T(8,128)}), f32[3072,256]{1,0:T(8,128)}) %all-gather.17.cloned.1.call-update) | async-done | bytes 3145744 | tf_op jit(solution)/shard_map/all_gather | solution.py:23
  844.8 11.4 convolution_bitcast_fusion
  856.3 32.3 %reduce-scatter.17.cloned.1.call-done = f32[96,256]{1,0:T(8,128)} async-done(((f32[768,256]{1,0:T(8,128)}), f32[96,256]{1,0:T(8,128)}) %reduce-scatter.17.cloned.1.call-update) | async-done | bytes 98320 | tf_op jit(solution)/shard_map/reduce_scatter | solution.py:27
  890.8 410.9 %all-reduce.3.cloned.1.call-done = f32[256,256]{1,0:T(8,128)} async-done(((f32[256,256]{1,0:T(8,128)}), f32[256,256]{1,0:T(8,128)}) %all-reduce.3.cloned.1.call-update) | async-done | bytes 262160 | tf_op jit(solution)/shard_map/psum | solution.py:14
  1301.7 89.6 %all-reduce.5.cloned.1.call-done = f32[256,256]{1,0:T(8,128)} async-done(((f32[256,256]{1,0:T(8,128)}), f32[256,256]{1,0:T(8,128)}) %all-reduce.5.cloned.1.call-update) | async-done | bytes 262160 | tf_op jit(solution)/shard_map/psum | solution.py:15
  1391.4 1.7 broadcast_multiply_fusion
  (46 shorter events, 7.0 us)
Async XLA Ops:
  7.2 106.7 %all-gather.7.cloned.1.call-start = ((), (), s32[]{:S(2)}) async-start(), calls=%async_computation.6 | async-start | bytes 3244032 | tf_op jit(solution)/shard_map/all_gather | solution.py:23
  7.9 149.8 %copy-start = (f32[96,256]{1,0:T(8,128)S(1)}, f32[96,256]{1,0:T(8,128)}, u32[]{:S(2)}) copy-start(f32[96,256]{1,0:T(8,128)} %param.3) | copy-start | bytes 294916
  7.9 149.8 %reduce-scatter.7.cloned.1.call-start = ((), (), s32[]{:S(2)}) async-start(), calls=%async_computation.7 | async-start | bytes 884736 | tf_op jit(solution)/shard_map/reduce_scatter | solution.py:27
  125.3 134.7 %all-gather.9.cloned.1.call-start = ((), (), s32[]{:S(2)}) async-start(), calls=%async_computation.8 | async-start | bytes 3244032 | tf_op jit(solution)/shard_map/all_gather | solution.py:23
  159.3 144.6 %copy-start.6 = (f32[96,256]{1,0:T(8,128)S(1)}, f32[96,256]{1,0:T(8,128)}, u32[]{:S(2)}) copy-start(f32[96,256]{1,0:T(8,128)} %reduce-scatter.7.cloned.1.call-done) | copy-start | bytes 294916
  159.3 144.6 %reduce-scatter.9.cloned.1.call-start = ((), (), s32[]{:S(2)}) async-start(), calls=%async_computation.9 | async-start | bytes 884736 | tf_op jit(solution)/shard_map/reduce_scatter | solution.py:27
  271.5 134.6 %all-gather.11.cloned.1.call-start = ((), (), s32[]{:S(2)}) async-start(), calls=%async_computation.10 | async-start | bytes 3244032 | tf_op jit(solution)/shard_map/all_gather | solution.py:23
  305.5 144.5 %copy-start.3 = (f32[96,256]{1,0:T(8,128)S(1)}, f32[96,256]{1,0:T(8,128)}, u32[]{:S(2)}) copy-start(f32[96,256]{1,0:T(8,128)} %multiply_subtract_fusion.4) | copy-start | bytes 294916
  305.5 144.5 %reduce-scatter.11.cloned.1.call-start = ((), (), s32[]{:S(2)}) async-start(), calls=%async_computation.11 | async-start | bytes 884736 | tf_op jit(solution)/shard_map/reduce_scatter | solution.py:27
  417.6 134.8 %all-gather.13.cloned.1.call-start = ((), (), s32[]{:S(2)}) async-start(), calls=%async_computation.12 | async-start | bytes 3244032 | tf_op jit(solution)/shard_map/all_gather | solution.py:23
  451.6 144.6 %copy-start.1 = (f32[96,256]{1,0:T(8,128)S(1)}, f32[96,256]{1,0:T(8,128)}, u32[]{:S(2)}) copy-start(f32[96,256]{1,0:T(8,128)} %multiply_subtract_fusion.3) | copy-start | bytes 294916
  451.6 144.6 %reduce-scatter.13.cloned.1.call-start = ((), (), s32[]{:S(2)}) async-start(), calls=%async_computation.13 | async-start | bytes 884736 | tf_op jit(solution)/shard_map/reduce_scatter | solution.py:27
  563.8 134.8 %all-gather.15.cloned.1.call-start = ((), (), s32[]{:S(2)}) async-start(), calls=%async_computation.14 | async-start | bytes 3244032 | tf_op jit(solution)/shard_map/all_gather | solution.py:23
  597.8 144.7 %copy-start.2 = (f32[96,256]{1,0:T(8,128)S(1)}, f32[96,256]{1,0:T(8,128)}, u32[]{:S(2)}) copy-start(f32[96,256]{1,0:T(8,128)} %multiply_subtract_fusion.2) | copy-start | bytes 294916
  597.8 144.7 %reduce-scatter.15.cloned.1.call-start = ((), (), s32[]{:S(2)}) async-start(), calls=%async_computation.15 | async-start | bytes 884736 | tf_op jit(solution)/shard_map/reduce_scatter | solution.py:27
  710.1 134.7 %all-gather.17.cloned.1.call-start = ((), (), s32[]{:S(2)}) async-start(), calls=%async_computation.16 | async-start | bytes 3244032 | tf_op jit(solution)/shard_map/all_gather | solution.py:23
  744.1 144.6 %copy-start.5 = (f32[96,256]{1,0:T(8,128)S(1)}, f32[96,256]{1,0:T(8,128)}, u32[]{:S(2)}) copy-start(f32[96,256]{1,0:T(8,128)} %multiply_subtract_fusion.1) | copy-start | bytes 294916
  744.1 144.6 %reduce-scatter.17.cloned.1.call-start = ((), (), s32[]{:S(2)}) async-start(), calls=%async_computation.17 | async-start | bytes 884736 | tf_op jit(solution)/shard_map/reduce_scatter | solution.py:27
  856.3 445.4 %all-reduce.3.cloned.1.call-start = ((), (), s32[]{:S(2)}) async-start(), calls=%async_computation.18 | async-start | bytes 524288 | tf_op jit(solution)/shard_map/psum | solution.py:14
  889.6 503.5 %copy-start.4 = (f32[96,256]{1,0:T(8,128)}, f32[96,256]{1,0:T(8,128)S(1)}, u32[]{:S(2)}) copy-start(f32[96,256]{1,0:T(8,128)S(1)} %multiply_subtract_fusion) | copy-start | bytes 294916
  890.8 500.6 %all-reduce.5.cloned.1.call-start = ((), (), s32[]{:S(2)}) async-start(), calls=%async_computation.19 | async-start | bytes 524288 | tf_op jit(solution)/shard_map/psum | solution.py:15
Sparse Core Ops, SparseCore 0:
  11.4 102.4 all-gather.6
  125.4 32.2 reduce-scatter.6
  161.7 98.3 all-gather.8
  271.6 32.2 reduce-scatter.8
  307.7 98.3 all-gather.10
  417.7 32.2 reduce-scatter.10
  454.0 98.3 all-gather.12
  564.0 32.2 reduce-scatter.12
  600.2 98.3 all-gather.14
  710.2 32.2 reduce-scatter.14
  746.5 98.3 all-gather.16
  856.4 32.2 reduce-scatter.16
  891.9 409.8 all-reduce.2
  1304.2 87.1 all-reduce.4
